TPU v7x, 32 devices: a whole 2x2x4 slice. The times are simulated.
32 devices in a mesh: dp: 16 (over z, y, x), mp: 2 (over core).
Axes of the slice: x: 2, y: 2, z: 4, core: 2. Of those that a mesh axis runs over, the one named last changes fastest.
Arguments:
- store_rows: bfloat16 [8192, 4096], P('dp', 'mp'), may hold values from -64 to 64
- norm_gain: bfloat16 [4096], replicated, may hold values from 0.099609375 to 1.8984375
- key_weight: bfloat16 [4096, 2048], P(None, 'mp'), may hold values from -0.09375 to 0.09375
- value_weight: bfloat16 [4096, 2048], P(None, 'mp'), may hold values from -0.09375 to 0.09375
- queries: bfloat16 [128, 2048], P('dp', 'mp'), may hold values from -300 to 300
- counts: int32 [16], replicated, may hold values from 1 to 8, 32 in all
- slot_plan: int32 [32], P('dp'), may hold values from 0 to 31, each once
Outputs:
- context: bfloat16 [128, 2048], P('dp', 'mp')
All inputs are finite; a program needn't handle non-finite values.
Results may differ from a plain program's by a relative error of at most 0.0091.
Values may be sent and summed in bfloat16 or wider, within the bound.
A program may use at most 64 MiB of HBM per device.

v0:
```python
import jax
import jax.numpy as jnp
from jax import lax
from jax.sharding import PartitionSpec as P

HEAD_DIM = 64
norm_eps = 1e-06
score_scale = 0.125
far_below = -1e30


def local(store_rows, norm_gain, key_weight, value_weight, queries, counts, slot_plan):
    full_width = norm_gain.shape[0]
    row_count = store_rows.shape[0]
    local_cols = store_rows.shape[1]
    head_cols = key_weight.shape[1]
    heads_here = head_cols // HEAD_DIM
    passages_here = slot_plan.shape[0]
    seq_len = row_count // passages_here
    gain_full = norm_gain.astype(jnp.float32)
    raw_rows = store_rows.astype(jnp.float32)
    own_gain = lax.dynamic_slice_in_dim(gain_full, lax.axis_index("mp") * local_cols, local_cols, 0)
    scaled = (raw_rows * own_gain[None, :]).astype(jnp.bfloat16)
    total_sq = lax.psum(jnp.sum(raw_rows * raw_rows, axis=1), "mp")
    shard_part = lax.all_gather(scaled, "mp", axis=1, tiled=True)
    key_acc = jnp.dot(shard_part, key_weight, preferred_element_type=jnp.float32)
    value_acc = jnp.dot(shard_part, value_weight, preferred_element_type=jnp.float32)
    inv_rms = lax.rsqrt(total_sq / full_width + norm_eps)
    key_rows = (key_acc * inv_rms[:, None]).astype(jnp.bfloat16)
    value_rows = (value_acc * inv_rms[:, None]).astype(jnp.bfloat16)
    ends = jnp.cumsum(counts)
    slot_question = jnp.sum((slot_plan[:, None] >= ends[None, :]).astype(jnp.int32), axis=1)
    num_questions = counts.shape[0]
    dec_len = queries.shape[0]
    gathered = lax.all_gather(queries, "dp", axis=0, tiled=True)
    query_table = gathered.reshape(num_questions, dec_len, heads_here, HEAD_DIM)
    slot_queries = jnp.take(query_table, slot_question, axis=0)
    key_blocks = key_rows.reshape(passages_here, seq_len, heads_here, HEAD_DIM)
    value_blocks = value_rows.reshape(passages_here, seq_len, heads_here, HEAD_DIM).astype(
        jnp.float32
    )
    scores = (
        jnp.einsum("pihd,pthd->piht", slot_queries, key_blocks, preferred_element_type=jnp.float32)
        * score_scale
    )
    slot_max = jnp.max(scores, axis=3)
    member = slot_question[None, :] == jnp.arange(num_questions, dtype=jnp.int32)[:, None]
    member_float = member.astype(jnp.float32)
    question_max = jnp.max(jnp.where(member[:, :, None, None], slot_max[None], far_below), axis=1)
    max_level = lax.pmax(question_max, "dp")
    slot_level = jnp.take(max_level, slot_question, axis=0)
    weights = jnp.exp(scores - slot_level[..., None])
    slot_den = jnp.sum(weights, axis=3)
    slot_num = jnp.einsum("piht,pthd->pihd", weights, value_blocks, precision=lax.Precision.HIGHEST)
    slot_num = slot_num.reshape(passages_here, dec_len, head_cols)
    numerator = jnp.einsum("qp,pik->qik", member_float, slot_num, precision=lax.Precision.HIGHEST)
    denominator = jnp.einsum("qp,pih->qih", member_float, slot_den, precision=lax.Precision.HIGHEST)
    numerator, denominator = (numerator, denominator)
    summed_num, summed_den = (
        lax.psum_scatter(numerator, "dp", scatter_dimension=0, tiled=True),
        lax.psum_scatter(denominator, "dp", scatter_dimension=0, tiled=True),
    )
    own_num = summed_num[0]
    own_den = summed_den[0]
    context = own_num.reshape(dec_len, heads_here, HEAD_DIM) / own_den[..., None]
    return context.reshape(dec_len, head_cols).astype(jnp.bfloat16)


def solution(mesh):
    placed = (P("dp", "mp"), P(), P(None, "mp"), P(None, "mp"), P("dp", "mp"), P(), P("dp"))
    return jax.shard_map(
        local, mesh=mesh, in_specs=placed, out_specs=P("dp", "mp"), check_vma=False
    )
```

profile of v0, /device:TPU:0, one launch (start us, length us, event | category | flops | bytes accessed | tf_op | source)
XLA Modules:
  0.0 241.7 jit_solution(15678639214267508043)
XLA Ops:
  6.5 0.7 dynamic-slice_convert_fusion
  7.2 3.5 %fusion.1 = (f32[512]{0:T(512)S(1)}, bf16[512,2048]{1,0:T(8,128)(2,1)}) fusion(bf16[512,2048]{1,0:T(8,128)(2,1)} %param.7, f32[2048]{0:T(1024)S(1)} %dynamic-slice_convert_fusion), kind=kLoop, calls=%fused_computation.5 | loop fusion | flops 5242368 | bytes 4204544 | tf_op jit(solution)/shard_map/reduce_sum | solution.py:24
  10.8 0.6 copy-done.1
  11.4 0.1 copy.36
  11.5 0.1 reduce
  11.7 0.2 fusion.23
  11.8 0.1 iota_compare_fusion
  11.9 0.1 copy.41
  12.0 43.8 %all_gather.7 = bf16[128,1024]{1,0:T(8,128)(2,1)S(1)} all-gather(bf16[8,1024]{1,0:T(8,128)(2,1)S(1)} %copy-done), channel_id=1, replica_groups=mesh['dp'=16,'mp'=2] {'dp'}, dimensions={0}, use_global_device_ids=true | all-gather | bytes 278528 | tf_op jit(solution)/shard_map/all_gather | solution.py:35
  55.8 0.3 reshape.86
  56.2 0.6 gather_fusion
  56.7 2.5 %psum.7 = f32[512]{0:T(512)S(1)} all-reduce(f32[512]{0:T(512)S(1)} %get-tuple-element.5), channel_id=1, replica_groups=mesh['dp'=16,'mp'=2] {'mp'}, use_global_device_ids=true, to_apply=%region_3.4 | all-reduce | flops 512 | bytes 4096 | tf_op jit(solution)/shard_map/psum | solution.py:24
  59.2 0.1 broadcast_select_fusion
  59.3 9.1 %multiply_convert_fusion.1 = bf16[512,1024]{1,0:T(8,128)(2,1)S(1)} fusion(bf16[512,4096]{1,0:T(8,128)(2,1)} %all-gather.2.cloned.1.call-done, bf16[4096,1024]{1,0:T(8,128)(2,1)} %param.10, f32[512]{0:T(512)S(1)} %add_rsqrt_fusion), kind=kOutput, calls=%fused_computation.11 | convolution fusion | flops 4296015872 | bytes 13633536 | tf_op jit(solution)/shard_map/dot_general | solution.py:27
  68.4 1.3 reshape.105
  69.8 9.1 %multiply_convert_fusion = bf16[512,1024]{1,0:T(8,128)(2,1)S(1)} fusion(bf16[512,4096]{1,0:T(8,128)(2,1)} %all-gather.2.cloned.1.call-done, bf16[4096,1024]{1,0:T(8,128)(2,1)} %param.9, f32[512]{0:T(512)S(1)} %add_rsqrt_fusion), kind=kOutput, calls=%fused_computation.10 | convolution fusion | flops 4296015872 | bytes 13633536 | tf_op jit(solution)/shard_map/dot_general | solution.py:26
  78.9 2.4 reshape.106
  81.3 2.3 fusion.25
  83.7 0.1 select_reduce_fusion
  83.8 72.0 %pmax.7 = f32[16,8,16]{2,1,0:T(8,128)S(1)} all-reduce(f32[16,8,16]{2,1,0:T(8,128)S(1)} %select_reduce_fusion), channel_id=1, replica_groups=mesh['dp'=16,'mp'=2] {'dp'}, use_global_device_ids=true, to_apply=%region_6.7 | all-reduce | flops 2048 | bytes 16384 | tf_op jit(solution)/shard_map/pmax | solution.py:50
  155.8 0.5 gather_fusion.1
  156.5 1.2 fusion.12
  157.8 0.1 reshape.107
  157.9 0.5 fusion.21
  158.4 1.1 copy.47
  159.5 0.6 dynamic-slice
  160.1 0.2 fusion.15
  160.4 0.3 fusion.19
  160.7 71.9 %all-reduce = f32[16,8,16]{2,1,0:T(8,128)S(1)} all-reduce(f32[16,8,16]{2,1,0:T(8,128)S(1)} %copy.49), channel_id=3, replica_groups=mesh['dp'=16,'mp'=2] {'dp'}, use_global_device_ids=true, to_apply=%region_9.10.clone | all-reduce | flops 2048 | bytes 16384
  232.7 0.6 dynamic-slice_bitcast_fusion
  233.4 0.1 div.23
  233.5 1.4 fusion.18
  (25 shorter events, 0.6 us)
Async XLA Ops:
  6.5 52.8 %all-gather.2.cloned.1.call-start = ((), (), s32[]{:S(2)}) async-start(), calls=%async_computation.1 | async-start | bytes 6291456 | tf_op jit(solution)/shard_map/all_gather | solution.py:25
  10.8 0.7 copy-start.1
  10.8 0.9 copy-start.2
  10.8 1.3 copy-start
  10.8 222.7 %reduce-scatter.2.cloned.1.call-start = ((), (), s32[]{:S(2)}) async-start(), calls=%async_computation.2 | async-start | bytes 557056 | tf_op jit(solution)/shard_map/reduce_scatter | solution.py:60
  157.7 1.8 copy-start.3
Sparse Core Ops, SparseCore 0:
  10.9 16.3 all-gather.1
  159.6 72.4 reduce-scatter.1
where the time goes:
time: 242 us
  blocking collectives  190 us (79%)
  matrix products  22.6 us (9%)
  between operations  13.6 us (6%)
  local copies, waits for them, and re-layouts  8.82 us (4%)
  other arithmetic  6.49 us (3%)
    pmax x1, blocking collectives, local(): max_level = lax.pmax(question_max, 'dp')  72 us
    unnamed x1, blocking collectives  71.9 us
    all_gather x1, blocking collectives, local(): gathered = lax.all_gather(queries, 'dp', axis=0, tiled=True)  43.8 us
    dot_general x1, matrix products, local(): jnp.dot(shard_part, key_weight, preferred_element_type=jnp.float32)  9.15 us
    dot_general x1, matrix products, local(): jnp.dot(shard_part, value_weight, preferred_element_type=jnp.float32)  9.15 us
  transfers between devices with their start and end apart: 2, of which 0 were waited for; matrix products, arithmetic and copies ran while one was open for 1% of the time, Pallas kernels for 0%

commit v1 on v0

--- a/solution.py
+++ b/solution.py
@@ -32,7 +32,14 @@
     slot_question = jnp.sum((slot_plan[:, None] >= ends[None, :]).astype(jnp.int32), axis=1)
     num_questions = counts.shape[0]
     dec_len = queries.shape[0]
-    gathered = lax.all_gather(queries, "dp", axis=0, tiled=True)
+    ways, here, turn = (lax.axis_size("dp"), lax.axis_index("dp"), queries.shape[0])
+    line, have = (queries, 1)
+    while have < ways:
+        line = jnp.concatenate(
+            [line, lax.ppermute(line, "dp", [(d, (d - have) % ways) for d in range(ways)])], axis=0
+        )
+        have = 2 * have
+    gathered = jnp.roll(line, here * turn, axis=0)
     query_table = gathered.reshape(num_questions, dec_len, heads_here, HEAD_DIM)
     slot_queries = jnp.take(query_table, slot_question, axis=0)
     key_blocks = key_rows.reshape(passages_here, seq_len, heads_here, HEAD_DIM)

time: 242 us -> 228 us (0.942)
  blocking collectives: 190 us -> 154 us
  waiting for transfers between devices: 0.05 us -> 13.7 us
  starting transfers between devices: 0.04 us -> 8.05 us
    all_gather x1 -> x0, blocking collectives: 43.8 us -> none  [local(): gathered = lax.all_gather(queries, 'dp', axis=0, tiled=True)]
    ppermute x0 -> x4, waiting for transfers between devices: none -> 13.7 us  [local(): lax.ppermute(line, 'dp', [(d, (d - have) % ways) for d in range(ways)])]
    ppermute x0 -> x4, starting transfers between devices: none -> 8.01 us  [local(): lax.ppermute(line, 'dp', [(d, (d - have) % ways) for d in range(ways)])]
    pmax x1, blocking collectives: 72 us -> 79.7 us  [local(): max_level = lax.pmax(question_max, 'dp')]
  transfers between devices with their start and end apart: 2 -> 6, of which waited for: 0 -> 3; matrix products, arithmetic and copies ran while one was open for 1% -> 2% of each run, Pallas kernels for 0% -> 0%
where the time goes in v1:
time: 228 us
  blocking collectives  154 us (68%)
  matrix products  22.6 us (10%)
  waiting for transfers between devices  13.7 us (6%)
  between operations  13.6 us (6%)
  local copies, waits for them, and re-layouts  8.97 us (4%)
  starting transfers between devices  8.05 us (4%)
  other arithmetic  6.51 us (3%)
    pmax x1, blocking collectives, local(): max_level = lax.pmax(question_max, 'dp')  79.7 us
    unnamed x1, blocking collectives  72 us
    ppermute x4, waiting for transfers between devices, local(): lax.ppermute(line, 'dp', [(d, (d - have) % ways) for d in range(ways)])  13.7 us
    dot_general x1, matrix products, local(): jnp.dot(shard_part, key_weight, preferred_element_type=jnp.float32)  9.15 us
    dot_general x1, matrix products, local(): jnp.dot(shard_part, value_weight, preferred_element_type=jnp.float32)  9.15 us
    ppermute x4, starting transfers between devices, local(): lax.ppermute(line, 'dp', [(d, (d - have) % ways) for d in range(ways)])  8.01 us
  transfers between devices with their start and end apart: 6, of which 3 were waited for; matrix products, arithmetic and copies ran while one was open for 2% of the time, Pallas kernels for 0%

profile of v1, /device:TPU:0, one launch (start us, length us, event | category | flops | bytes accessed | tf_op | source)
XLA Modules:
  0.0 227.7 jit_solution(8624072191167993610)
XLA Ops:
  6.5 0.7 dynamic-slice_convert_fusion
  7.2 3.5 %fusion.1 = (f32[512]{0:T(512)S(1)}, bf16[512,2048]{1,0:T(8,128)(2,1)}) fusion(bf16[512,2048]{1,0:T(8,128)(2,1)} %param.7, f32[2048]{0:T(1024)S(1)} %dynamic-slice_convert_fusion), kind=kLoop, calls=%fused_computation.5 | loop fusion | flops 5242368 | bytes 4204544 | tf_op jit(solution)/shard_map/reduce_sum | solution.py:24
  10.8 0.6 copy-done
  11.5 6.9 %collective-permute-start = (bf16[8,1024]{1,0:T(8,128)(2,1)S(1)}, bf16[8,1024]{1,0:T(8,128)(2,1)S(1)}, u32[]{:S(2)}, u32[]{:S(2)}) collective-permute-start(bf16[8,1024]{1,0:T(8,128)(2,1)S(1)} %copy-done), channel_id=1, source_target_pairs={{0,30},{2,0},{4,2},{6,4},{8,6},{10,8},{12,10},{14,12},{16,14},{18,... | collective-permute-start | bytes 49160 | tf_op jit(solution)/shard_map/ppermute | solution.py:39
  18.5 0.1 reduce
  18.7 2.5 %psum.7 = f32[512]{0:T(512)S(1)} all-reduce(f32[512]{0:T(512)S(1)} %get-tuple-element.5), channel_id=1, replica_groups=mesh['dp'=16,'mp'=2] {'mp'}, use_global_device_ids=true, to_apply=%region_3.4 | all-reduce | flops 512 | bytes 4096 | tf_op jit(solution)/shard_map/psum | solution.py:24
  21.1 0.2 fusion.23
  21.4 0.6 collective-permute-start.1
  22.1 3.3 %collective-permute-done.1 = bf16[16,1024]{1,0:T(8,128)(2,1)S(1)} collective-permute-done((bf16[16,1024]{1,0:T(8,128)(2,1)S(1)}, bf16[16,1024]{1,0:T(8,128)(2,1)S(1)}, u32[]{:S(2)}, u32[]{:S(2)}) %collective-permute-start.1) | collective-permute-done | bytes 32800 | tf_op jit(solution)/shard_map/ppermute | solution.py:39
  25.4 0.4 collective-permute-start.2
  25.8 3.8 %collective-permute-done.2 = bf16[32,1024]{1,0:T(8,128)(2,1)S(1)} collective-permute-done((bf16[32,1024]{1,0:T(8,128)(2,1)S(1)}, bf16[32,1024]{1,0:T(8,128)(2,1)S(1)}, u32[]{:S(2)}, u32[]{:S(2)}) %collective-permute-start.2) | collective-permute-done | bytes 65568 | tf_op jit(solution)/shard_map/ppermute | solution.py:39
  29.8 6.6 %collective-permute-done.3 = bf16[64,1024]{1,0:T(8,128)(2,1)S(1)} collective-permute-done((bf16[64,1024]{1,0:T(8,128)(2,1)S(1)}, bf16[64,1024]{1,0:T(8,128)(2,1)S(1)}, u32[]{:S(2)}, u32[]{:S(2)}) %collective-permute-start.3) | collective-permute-done | bytes 131104 | tf_op jit(solution)/shard_map/ppermute | solution.py:39
  36.5 0.3 reshape.86
  36.8 0.6 gather_fusion
  37.5 9.1 %multiply_convert_fusion.1 = bf16[512,1024]{1,0:T(8,128)(2,1)S(1)} fusion(bf16[512,4096]{1,0:T(8,128)(2,1)} %all-gather.2.cloned.1.call-done, bf16[4096,1024]{1,0:T(8,128)(2,1)} %param.10, f32[512]{0:T(512)S(1)} %add_rsqrt_fusion), kind=kOutput, calls=%fused_computation.11 | convolution fusion | flops 4296015872 | bytes 13633536 | tf_op jit(solution)/shard_map/dot_general | solution.py:27
  46.6 1.3 reshape.105
  48.0 9.1 %multiply_convert_fusion = bf16[512,1024]{1,0:T(8,128)(2,1)S(1)} fusion(bf16[512,4096]{1,0:T(8,128)(2,1)} %all-gather.2.cloned.1.call-done, bf16[4096,1024]{1,0:T(8,128)(2,1)} %param.9, f32[512]{0:T(512)S(1)} %add_rsqrt_fusion), kind=kOutput, calls=%fused_computation.10 | convolution fusion | flops 4296015872 | bytes 13633536 | tf_op jit(solution)/shard_map/dot_general | solution.py:26
  57.1 2.4 %reshape.106 = bf16[2,256,16,64]{3,2,1,0:T(8,128)(2,1)} reshape(bf16[512,1024]{1,0:T(8,128)(2,1)S(1)} %multiply_convert_fusion) | data formatting | bytes 2097152 | tf_op jit(solution)/shard_map/reshape | solution.py:45
  59.5 2.3 %fusion.25 = (f32[2,8,16]{1,2,0:T(8,128)S(1)}, f32[2,8,16,256]{3,1,2,0:T(8,128)S(1)}) fusion(bf16[2,8,16,64]{3,2,1,0:T(8,128)(2,1)S(1)} %broadcast_select_fusion, bf16[2,256,16,64]{3,2,1,0:T(8,128)(2,1)} %reshape.106), kind=kOutput, calls=%fused_computation.53 | convolution fusion | flops 8519424 | bytes 1344512 | tf_op jit(solution)/shard_map/pihd,pthd->piht/dot_general | solution.py:50
  61.9 0.1 select_reduce_fusion
  62.0 79.7 %pmax.7 = f32[16,8,16]{2,1,0:T(8,128)S(1)} all-reduce(f32[16,8,16]{2,1,0:T(8,128)S(1)} %select_reduce_fusion), channel_id=1, replica_groups=mesh['dp'=16,'mp'=2] {'dp'}, use_global_device_ids=true, to_apply=%region_6.7 | all-reduce | flops 2048 | bytes 16384 | tf_op jit(solution)/shard_map/pmax | solution.py:57
  141.7 0.5 gather_fusion.1
  142.5 1.2 fusion.12
  143.7 0.1 reshape.107
  143.8 0.5 fusion.21
  144.3 1.1 copy.47
  145.5 0.6 dynamic-slice
  146.1 0.2 fusion.15
  146.3 0.3 fusion.19
  146.7 72.0 %all-reduce = f32[16,8,16]{2,1,0:T(8,128)S(1)} all-reduce(f32[16,8,16]{2,1,0:T(8,128)S(1)} %copy.49), channel_id=3, replica_groups=mesh['dp'=16,'mp'=2] {'dp'}, use_global_device_ids=true, to_apply=%region_9.10.clone | all-reduce | flops 2048 | bytes 16384
  218.7 0.6 dynamic-slice_bitcast_fusion
  219.5 1.4 fusion.18
  (46 shorter events, 1.2 us)
Async XLA Ops:
  6.5 30.9 %all-gather.2.cloned.1.call-start = ((), (), s32[]{:S(2)}) async-start(), calls=%async_computation.1 | async-start | bytes 6291456 | tf_op jit(solution)/shard_map/all_gather | solution.py:25
  10.8 0.7 copy-start
  10.8 7.7 %copy-start.1 = (s32[16]{0:T(128)S(1)}, s32[16]{0:T(128)}, u32[]{:S(2)}) copy-start(s32[16]{0:T(128)} %param.12) | copy-start | bytes 196
  10.8 10.4 %copy-start.2 = (s32[2]{0:T(128)S(1)}, s32[2]{0:T(128)}, u32[]{:S(2)}) copy-start(s32[2]{0:T(128)} %param.13) | copy-start | bytes 28
  10.8 208.7 %reduce-scatter.2.cloned.1.call-start = ((), (), s32[]{:S(2)}) async-start(), calls=%async_computation.2 | async-start | bytes 557056 | tf_op jit(solution)/shard_map/reduce_scatter | solution.py:67
  11.5 9.9 %collective-permute-start = (bf16[8,1024]{1,0:T(8,128)(2,1)S(1)}, bf16[8,1024]{1,0:T(8,128)(2,1)S(1)}, u32[]{:S(2)}, u32[]{:S(2)}) collective-permute-start(bf16[8,1024]{1,0:T(8,128)(2,1)S(1)} %copy-done), channel_id=1, source_target_pairs={{0,30},{2,0},{4,2},{6,4},{8,6},{10,8},{12,10},{14,12},{16,14},{18,... | collective-permute-start | bytes 49160 | tf_op jit(solution)/shard_map/ppermute | solution.py:39
  21.4 4.0 %collective-permute-start.1 = (bf16[16,1024]{1,0:T(8,128)(2,1)S(1)}, bf16[16,1024]{1,0:T(8,128)(2,1)S(1)}, u32[]{:S(2)}, u32[]{:S(2)}) collective-permute-start(bf16[16,1024]{1,0:T(8,128)(2,1)S(1)} %pad_maximum_fusion.2), channel_id=1, source_target_pairs={{0,28},{2,30},{4,0},{6,2},{8,4},{10,6},{12,8},{14,10},{16,12},{18,... | collective-permute-start | bytes 98312 | tf_op jit(solution)/shard_map/ppermute | solution.py:39
  25.4 4.3 %collective-permute-start.2 = (bf16[32,1024]{1,0:T(8,128)(2,1)S(1)}, bf16[32,1024]{1,0:T(8,128)(2,1)S(1)}, u32[]{:S(2)}, u32[]{:S(2)}) collective-permute-start(bf16[32,1024]{1,0:T(8,128)(2,1)S(1)} %pad_maximum_fusion.1), channel_id=1, source_target_pairs={{0,24},{2,26},{4,28},{6,30},{8,0},{10,2},{12,4},{14,6},{16,8},{18,... | collective-permute-start | bytes 196616 | tf_op jit(solution)/shard_map/ppermute | solution.py:39
  29.7 6.7 %collective-permute-start.3 = (bf16[64,1024]{1,0:T(8,128)(2,1)S(1)}, bf16[64,1024]{1,0:T(8,128)(2,1)S(1)}, u32[]{:S(2)}, u32[]{:S(2)}) collective-permute-start(bf16[64,1024]{1,0:T(8,128)(2,1)S(1)} %pad_maximum_fusion), channel_id=1, source_target_pairs={{0,16},{2,18},{4,20},{6,22},{8,24},{10,26},{12,28},{14,30},{16,0},... | collective-permute-start | bytes 393224 | tf_op jit(solution)/shard_map/ppermute | solution.py:39
  143.7 1.8 copy-start.3
Sparse Core Ops, SparseCore 0:
  10.9 16.3 all-gather.1
  145.6 72.4 reduce-scatter.1
